TPU v7x, 32 devices: a whole 2x2x4 slice. The times are simulated.
32 devices in a mesh: groups: 2 (over y), rows: 4 (over x, core), cols: 4 (over z).
Axes of the slice: x: 2, y: 2, z: 4, core: 2. Of those that a mesh axis runs over, the one named last changes fastest.
Arguments:
- q_fresh: bfloat16 [64, 128, 1536], P(('groups', 'rows'), 'cols'), parts along dimension 0, may hold values from -33 to 33
- k_fresh: bfloat16 [64, 128, 1536], P(('groups', 'rows'), 'cols'), parts along dimension 0, may hold values from -6.5 to 6.5
- v_fresh: bfloat16 [64, 128, 1536], P(('groups', 'rows'), 'cols'), parts along dimension 0, may hold values from -6 to 6
- k_stale: bfloat16 [64, 128, 1536], P(('groups', 'rows'), 'cols'), parts along dimension 0, may hold values from -6.375 to 6.375
- v_stale: bfloat16 [64, 128, 1536], P(('groups', 'rows'), 'cols'), parts along dimension 0, may hold values from -6 to 6
- text_k: bfloat16 [1024, 1536], P(('groups', 'rows', 'cols')), parts along dimension 0, may hold values from -6.375 to 6.375
- text_v: bfloat16 [1024, 1536], P(('groups', 'rows', 'cols')), parts along dimension 0, may hold values from -6 to 6
- conv_w: float32 [3, 3, 1536], replicated, may hold values from -0.8 to 0.8
- reads: int32 [8, 4, 2], P(('groups', 'rows'), 'cols'), parts along dimension 0, may hold values from 0 to 7, as said below
- pattern: int32 [16, 4, 2], P(('groups', 'rows'), 'cols'), parts along dimension 0, may hold values from 0 to 3, as said below
- text_blocks: int32 [16, 4, 2], P(('groups', 'rows'), 'cols'), parts along dimension 0, may hold values from 0 to 3, all different within a row
Outputs:
- attended: float32 [64, 128, 1536], P(('groups', 'rows'), 'cols'), parts along dimension 0
There are 2 independent parts, one for each index of `groups`. A program takes and returns all parts, laid end to end along the dimension named above; an argument that names none is the same for every part. Nothing has to cross between parts.
Inputs may be any that keep to these rules, and one draw needn't show every extreme that they name: `reads`: entry f of device (r, c) names a block row of column strip c; the device row of that block row (the entry // 2) differs from r and from those of the device's other entries. `pattern`: each row lists 2 distinct slots; the row of block row i always lists slot i % 2, and every slot from 2 up is listed by some block of its device.
All inputs are finite; a program needn't handle non-finite values.
Results may differ from a plain program's by a relative error of at most 0.00075.
Values may be sent and summed in bfloat16 or wider, within the bound.
No kernel may reach another device: no remote copies, remote signals or barrier semaphores. Data moves between devices by JAX's collectives and lax.ppermute only.
A program may use at most 192 MiB of HBM per device.

v0:
```python
import math
import jax
import jax.numpy as jnp
from jax import lax
from jax.sharding import PartitionSpec as P

HEAD_DIM = 128
BLOCK_ROWS = 4
BLOCK_COLS = 32


def extended(cells, sides, width):
    for axis, dim in sides:
        count = lax.axis_size(axis)
        ends = count - 1
        head = lax.slice_in_dim(cells, 0, width, axis=dim)
        tail = lax.slice_in_dim(cells, cells.shape[dim] - width, cells.shape[dim], axis=dim)
        cells = jnp.concatenate(
            [
                lax.ppermute(tail, axis, [(i, (i + 1) % count) for i in range(ends)]),
                cells,
                lax.ppermute(head, axis, [((i + 1) % count, i) for i in range(ends)]),
            ],
            axis=dim,
        )
    return cells


def split_heads(flat_rows):
    return flat_rows.reshape(flat_rows.shape[:-1] + (flat_rows.shape[-1] // HEAD_DIM, HEAD_DIM))


def attend(softmax_state, queries, key_blocks, value_blocks, allowed):
    old_peak, old_total, old_summed = softmax_state
    scores = jnp.einsum(
        "bqhd,nkhd->bhqnk", queries, key_blocks, preferred_element_type=jnp.float32
    ) * (1.0 / math.sqrt(HEAD_DIM))
    scores = jnp.where(allowed[:, None, None, :, None], scores, -1e30)
    new_peak = jnp.maximum(old_peak, jnp.max(scores, axis=(3, 4)))
    weights = jnp.exp(scores - new_peak[:, :, :, None, None]).astype(jnp.bfloat16)
    factor = jnp.exp(old_peak - new_peak)
    new_total = old_total * factor + jnp.sum(weights.astype(jnp.float32), axis=(3, 4))
    product = jnp.einsum(
        "bhqnk,nkhd->bqhd", weights, value_blocks, preferred_element_type=jnp.float32
    )
    new_summed = old_summed * jnp.transpose(factor, (0, 2, 1))[:, :, :, None] + product
    return (new_peak, new_total, new_summed)


def body(
    q_fresh, k_fresh, v_fresh, k_stale, v_stale, text_k, text_v, conv_w, reads, pattern, text_blocks
):
    rows_here, cols_here, feature_width = q_fresh.shape
    per_block = BLOCK_ROWS * BLOCK_COLS
    blocks_here = rows_here // BLOCK_ROWS
    head_count = feature_width // HEAD_DIM

    def as_blocks(grid_values):
        return split_heads(grid_values.reshape(blocks_here, per_block, feature_width))

    queries = as_blocks(q_fresh)
    own_keys = as_blocks(k_fresh)
    own_values = as_blocks(v_fresh)
    text_keys, text_values = (
        lax.all_gather(text_k, ("rows", "cols"), axis=0, tiled=True),
        lax.all_gather(text_v, ("rows", "cols"), axis=0, tiled=True),
    )
    text_count = text_keys.shape[0] // per_block
    text_keys = split_heads(text_keys.reshape(text_count, per_block, feature_width))
    text_values = split_heads(text_values.reshape(text_count, per_block, feature_width))
    wanted = pattern[:, 0, :]
    fetch_rows = reads[0, 0, :]
    fetch_count = fetch_rows.shape[0]
    slot_count = blocks_here + fetch_count
    slot_mask = jnp.any(
        wanted[:, :, None] == jnp.arange(slot_count, dtype=jnp.int32)[None, None, :], axis=1
    )
    text_mask = jnp.any(
        text_blocks[:, 0, :, None] == jnp.arange(text_count, dtype=jnp.int32)[None, None, :], axis=1
    )
    start_state = (
        jnp.full((blocks_here, head_count, per_block), -1e30, jnp.float32),
        jnp.zeros((blocks_here, head_count, per_block), jnp.float32),
        jnp.zeros((blocks_here, per_block, head_count, HEAD_DIM), jnp.float32),
    )
    softmax_state = attend(
        start_state,
        queries,
        jnp.concatenate([own_keys, text_keys], axis=0),
        jnp.concatenate([own_values, text_values], axis=0),
        jnp.concatenate([slot_mask[:, :blocks_here], text_mask], axis=1),
    )
    chosen = jnp.where(
        wanted >= blocks_here, fetch_rows[jnp.clip(wanted - blocks_here, 0, fetch_count - 1)], -1
    )
    piece_keys = lax.all_gather(as_blocks(k_stale), "rows", axis=0, tiled=True)
    piece_values = lax.all_gather(as_blocks(v_stale), "rows", axis=0, tiled=True)
    piece_count = piece_keys.shape[0]
    block_rows = jnp.arange(piece_count, dtype=jnp.int32)
    piece_mask = jnp.any(chosen[:, :, None] == block_rows[None, None, :], axis=1)
    softmax_state = attend(softmax_state, queries, piece_keys, piece_values, piece_mask)
    final_peak, final_total, final_summed = softmax_state
    mixed_rows = final_summed / jnp.transpose(final_total, (0, 2, 1))[:, :, :, None]
    attention = mixed_rows.reshape(rows_here, cols_here, feature_width)
    rims = extended(v_fresh, (("rows", 0), ("cols", 1)), 1)
    position_term = jnp.zeros((rows_here, cols_here, feature_width), jnp.float32)
    for row_tap in range(3):
        for col_tap in range(3):
            position_term = position_term + conv_w[row_tap, col_tap] * rims[
                row_tap : row_tap + rows_here, col_tap : col_tap + cols_here
            ].astype(jnp.float32)
    return attention + position_term


def solution(mesh):
    in_specs = (
        P(("groups", "rows"), "cols", None),
        P(("groups", "rows"), "cols", None),
        P(("groups", "rows"), "cols", None),
        P(("groups", "rows"), "cols", None),
        P(("groups", "rows"), "cols", None),
        P(("groups", "rows", "cols"), None),
        P(("groups", "rows", "cols"), None),
        P(),
        P(("groups", "rows"), "cols", None),
        P(("groups", "rows"), "cols", None),
        P(("groups", "rows"), "cols", None),
    )
    out_specs = P(("groups", "rows"), "cols", None)
    return jax.shard_map(body, mesh=mesh, in_specs=in_specs, out_specs=out_specs, check_vma=False)
```

profile of v0, /device:TPU:0, one launch (start us, length us, event | category | flops | bytes accessed | tf_op | source)
XLA Modules:
  0.0 184.2 jit_solution(10982115010975947880)
XLA Ops:
  6.5 0.0 all-gather.5.cloned.1.call-start
  6.5 0.7 all-gather.5.cloned.1.call-update
  7.3 0.0 all-gather.7.cloned.1.call-start
  7.3 0.7 all-gather.7.cloned.1.call-update
  8.0 0.0 all-gather.9.cloned.1.call-start
  8.1 1.6 reshape_reshape.26
  9.7 0.0 copy-start.2
  9.7 0.0 copy-start.6
  9.7 1.1 copy.41
  10.8 0.0 all-gather.9.cloned.1.call-update
  10.8 0.0 all-gather.11.cloned.1.call-start
  10.9 0.0 copy-done.2
  10.9 2.4 %collective-permute-start = (bf16[1,32,1536]{2,1,0:T(8,128)(2,1)S(1)}, bf16[1,32,1536]{2,1,0:T(8,128)(2,1)S(1)}, u32[]{:S(2)}, u32[]{:S(2)}) collective-permute-start(bf16[1,32,1536]{2,1,0:T(8,128)(2,1)S(1)} %get-tuple-element.19), channel_id=1, source_target_pairs={{0,4},{4,8},{8,12},{1,5},{5,9},{9,13},{2,6},{6,10},{10,14},{3,7},{... | collective-permute-start | bytes 294920 | tf_op jit(solution)/shard_map/ppermute | solution.py:20
  13.3 1.3 collective-permute-start.1
  14.6 0.0 copy-done.6
  14.6 0.5 reshape_reshape.27
  15.1 1.1 copy.43
  16.3 0.0 all-gather.11.cloned.1.call-update
  16.3 0.5 reshape_reshape.24
  16.8 0.1 copy-done.23
  16.9 0.1 compare_reduce_fusion.2
  17.0 0.1 compare_reduce_fusion.1
  17.1 0.1 pad_add_fusion
  17.2 0.1 copy.31
  17.3 0.1 copy-done.7
  17.4 1.5 reshape_reshape.23
  19.0 1.6 reshape_reshape.21
  20.6 1.2 copy.33
  21.8 0.1 reshape.56
  21.9 0.0 copy-done
  21.9 0.6 gather_fusion
  22.5 0.1 reshape.55
  22.6 0.1 compare_reduce_fusion
  22.7 0.1 copy.40
  22.8 1.5 copy.37
  24.3 0.7 slice_reduce_fusion.8
  25.1 0.0 collective-permute-done
  25.1 0.1 constant_dynamic-update-slice_fusion.1
  25.2 0.0 collective-permute-done.1
  25.2 1.0 copy-done.5
  26.2 0.1 fusion.36
  26.3 4.3 %collective-permute-start.2 = (bf16[10,1,1536]{2,1,0:T(2,128)(2,1)S(1)}, bf16[10,1,1536]{2,1,0:T(2,128)(2,1)S(1)}, u32[]{:S(2)}, u32[]{:S(2)}) collective-permute-start(bf16[10,1,1536]{2,1,0:T(2,128)(2,1)S(1)} %get-tuple-element.16), channel_id=1, source_target_pairs={{0,1},{1,2},{2,3},{4,5},{5,6},{6,7},{8,9},{9,10},{10,11},{12,13},{... | collective-permute-start | bytes 92168 | tf_op jit(solution)/shard_map/ppermute | solution.py:20
  30.6 1.5 collective-permute-start.3
  32.1 20.0 %all-gather.5.cloned.1.call-done = bf16[512,1536]{1,0:T(8,128)(2,1)} async-done(((bf16[32,1536]{1,0:T(8,128)(2,1)}), bf16[512,1536]{1,0:T(8,128)(2,1)}) %all-gather.5.cloned.1.call-update) | async-done | bytes 1572880 | tf_op jit(solution)/shard_map/all_gather | solution.py:65
  52.1 2.9 %reshape.71 = bf16[4,128,12,128]{3,2,1,0:T(8,128)(2,1)S(1)} reshape(bf16[512,1536]{1,0:T(8,128)(2,1)} %all-gather.5.cloned.1.call-done) | data formatting | bytes 3145728 | tf_op jit(solution)/shard_map/reshape;reshape | solution.py:30
  55.0 1.6 copy.34
  56.5 36.5 %all-gather.7.cloned.1.call-done = bf16[512,1536]{1,0:T(8,128)(2,1)} async-done(((bf16[32,1536]{1,0:T(8,128)(2,1)}), bf16[512,1536]{1,0:T(8,128)(2,1)}) %all-gather.7.cloned.1.call-update) | async-done | bytes 1572880 | tf_op jit(solution)/shard_map/all_gather | solution.py:66
  93.0 2.9 %reshape.72 = bf16[4,128,12,128]{3,2,1,0:T(8,128)(2,1)S(1)} reshape(bf16[512,1536]{1,0:T(8,128)(2,1)} %all-gather.7.cloned.1.call-done) | data formatting | bytes 3145728 | tf_op jit(solution)/shard_map/reshape;reshape | solution.py:30
  95.9 2.8 %copy.38 = bf16[4,128,12,128]{1,3,0,2:T(8,128)(2,1)} copy(bf16[4,128,12,128]{3,2,1,0:T(8,128)(2,1)S(1)} %reshape.72) | data formatting | bytes 3145728 | tf_op jit(solution)/shard_map/reshape;reshape | solution.py:30
  98.6 7.3 %fusion.1 = (f32[2,12,128]{2,0,1:T(2,128)S(1)}, f32[12,6,128,2,128]{4,2,3,1,0:T(8,128)}) fusion(pred[2,6]{0,1:T(8,128)(4,1)S(1)} %copy.31, bf16[2,128,12,128,1]{3,2,1,0,4:T(8,128)(2,1)} %bitcast.98, bf16[4,128,12,128]{3,1,0,2:T(8,128)(2,1)} %copy.34, bf16[2,128,12,128]{3,1,0,2:T(8,128)(2,1)} %copy.33), kind=kOutput, calls=%fused_computation.8 | convolution fusion | flops 615773184 | bytes 12595212 | tf_op jit(solution)/shard_map/bqhd,nkhd->bhqnk/dot_general | solution.py:35
  106.0 16.1 %all-gather.9.cloned.1.call-done = bf16[8,128,12,128]{3,1,0,2:T(8,128)(2,1)} async-done(((bf16[2,128,12,128]{3,1,0,2:T(8,128)(2,1)}), bf16[8,128,12,128]{3,1,0,2:T(8,128)(2,1)}) %all-gather.9.cloned.1.call-update) | async-done | bytes 3145744 | tf_op jit(solution)/shard_map/all_gather | solution.py:96
  122.0 3.6 %fusion = (f32[2,12,128]{2,0,1:T(2,128)S(1)}, f32[12,8,128,2,128]{4,2,3,1,0:T(8,128)S(1)}) fusion(pred[2,8]{0,1:T(8,128)(4,1)S(1)} %copy.40, bf16[2,128,12,128,1]{3,2,1,0,4:T(8,128)(2,1)S(1)} %bitcast.99, bf16[8,128,12,128]{3,1,0,2:T(8,128)(2,1)} %all-gather.9.cloned.1.call-done), kind=kOutput, calls=%fused_computation.4 | convolution fusion | flops 814740480 | bytes 16527376 | tf_op jit(solution)/shard_map/bqhd,nkhd->bhqnk/dot_general | solution.py:35
  125.6 0.0 copy-start.1
  125.6 10.4 %convert_reduce_fusion.1 = f32[2,12,128]{2,0,1:T(2,128)S(1)} fusion(f32[2,12,128]{2,0,1:T(2,128)S(1)} %get-tuple-element.21, f32[12,6,128,2,128]{4,2,3,1,0:T(8,128)} %get-tuple-element.24, pred[2,6]{0,1:T(8,128)(4,1)S(1)} %copy.31), kind=kLoop, calls=%fused_computation.6 | loop fusion | flops 14152704 | bytes 9461772 | tf_op jit(solution)/shard_map/reduce_sum | solution.py:42
  136.0 2.6 %convert_reduce_fusion = f32[2,12,128]{2,0,1:T(2,128)S(1)} fusion(f32[2,12,128]{2,0,1:T(2,128)S(1)} %get-tuple-element.22, f32[12,8,128,2,128]{4,2,3,1,0:T(8,128)S(1)} %get-tuple-element.26, pred[2,8]{0,1:T(8,128)(4,1)S(1)} %copy.40), kind=kLoop, calls=%fused_computation.2 | loop fusion | flops 18871296 | bytes 12607504 | tf_op jit(solution)/shard_map/reduce_sum | solution.py:42
  138.6 0.6 bitcast_add_fusion.2
  139.3 12.7 %all-gather.11.cloned.1.call-done = bf16[8,128,12,128]{3,1,0,2:T(8,128)(2,1)} async-done(((bf16[2,128,12,128]{3,1,0,2:T(8,128)(2,1)}), bf16[8,128,12,128]{3,1,0,2:T(8,128)(2,1)}) %all-gather.11.cloned.1.call-update) | async-done | bytes 3145744 | tf_op jit(solution)/shard_map/all_gather | solution.py:97
  152.0 8.5 %fusion.2 = f32[12,2,128,128,1]{2,3,1,4,0:T(8,128)S(1)} fusion(bf16[8,128,12,128]{3,1,0,2:T(8,128)(2,1)} %all-gather.11.cloned.1.call-done, f32[12,8,128,2,128]{4,2,3,1,0:T(8,128)} %copy-done.1, f32[2,12,128]{2,0,1:T(2,128)S(1)} %get-tuple-element.22, pred[2,8]{0,1:T(8,128)(4,1)} %copy-done.22), kind=kOutput, calls=%fused_computation.9 | convolution fusion | flops 817889280 | bytes 17313808 | tf_op jit(solution)/shard_map/bhqnk,nkhd->bqhd/dot_general | solution.py:43
  160.5 7.3 %fusion.14 = f32[2,128,12,128]{1,3,0,2:T(8,128)} fusion(f32[12,2,128,128,1]{2,3,1,4,0:T(8,128)S(1)} %fusion.2, bf16[4,128,12,128]{1,3,0,2:T(8,128)(2,1)S(1)} %copy-done.4, bf16[2,128,12,128]{1,3,0,2:T(8,128)(2,1)S(1)} %copy-done.8, f32[2,128,12]{1,0,2:T(2,128)S(1)} %copy-done.19, f32[2,128,12]{1,0,2:T(2,128)S(1)} %copy-done.20, ...), kind=kOutput, calls=%fused_computation.27 | convolution fusion | flops 619708416 | bytes 14991372 | tf_op jit(solution)/shard_map/bhqnk,nkhd->bqhd/dot_general | solution.py:43
  167.9 2.2 %copy.46 = f32[2,128,12,128]{3,2,1,0:T(8,128)S(1)} copy(f32[2,128,12,128]{1,3,0,2:T(8,128)} %fusion.14) | data formatting | bytes 3145728 | tf_op jit(solution)/shard_map/div | solution.py:103
  170.1 1.4 reshape.53
  171.5 0.0 collective-permute-done.2
  171.5 0.0 collective-permute-done.3
  171.6 6.0 %add_add_fusion = f32[8,32,1536]{2,1,0:T(8,128)} fusion(f32[8,32,1536]{2,1,0:T(8,128)} %reshape.53, bf16[8,32,1536]{2,1,0:T(8,128)(2,1)S(1)} %copy-done.2, bf16[10,32,1536]{2,1,0:T(8,128)(2,1)} %copy-done.5, bf16[10,1,1536]{2,1,0:T(2,128)(2,1)} %collective-permute-done.3, bf16[10,1,1536]{2,1,0:T(2,128)(2,1)S(1)} %collective-permute-done.2, ...), kind=kLoop, calls=%fused_computation.30 | loop fusion | flops 20054016 | bytes 5228544 | tf_op jit(solution)/shard_map/add | solution.py:112
  (53 shorter events, 0.2 us)
Async XLA Ops:
  6.5 15.3 %copy-start = (s32[1,1,2]{2,1,0:T(1,128)S(1)}, s32[1,1,2]{2,1,0:T(1,128)}, u32[]{:S(2)}) copy-start(s32[1,1,2]{2,1,0:T(1,128)} %param.19) | copy-start | bytes 28
  6.5 45.5 %all-gather.5.cloned.1.call-start = ((), (), s32[]{:S(2)}) async-start(), calls=%async_computation | async-start | bytes 1671168 | tf_op jit(solution)/shard_map/all_gather | solution.py:65
  7.3 85.7 %all-gather.7.cloned.1.call-start = ((), (), s32[]{:S(2)}) async-start(), calls=%async_computation.1 | async-start | bytes 1671168 | tf_op jit(solution)/shard_map/all_gather | solution.py:66
  8.0 114.0 %all-gather.9.cloned.1.call-start = ((), (), s32[]{:S(2)}) async-start(), calls=%async_computation.2 | async-start | bytes 3932160 | tf_op jit(solution)/shard_map/all_gather | solution.py:96
  9.7 1.2 copy-start.2
  9.7 4.9 %copy-start.6 = (bf16[8,32,1536]{2,1,0:T(8,128)(2,1)S(1)}, bf16[8,32,1536]{2,1,0:T(8,128)(2,1)}, u32[]{:S(2)}) copy-start(bf16[8,32,1536]{2,1,0:T(8,128)(2,1)} %param.15) | copy-start | bytes 2359300
  10.8 141.2 %all-gather.11.cloned.1.call-start = ((), (), s32[]{:S(2)}) async-start(), calls=%async_computation.3 | async-start | bytes 3932160 | tf_op jit(solution)/shard_map/all_gather | solution.py:97
  10.9 14.2 %collective-permute-start = (bf16[1,32,1536]{2,1,0:T(8,128)(2,1)S(1)}, bf16[1,32,1536]{2,1,0:T(8,128)(2,1)S(1)}, u32[]{:S(2)}, u32[]{:S(2)}) collective-permute-start(bf16[1,32,1536]{2,1,0:T(8,128)(2,1)S(1)} %get-tuple-element.19), channel_id=1, source_target_pairs={{0,4},{4,8},{8,12},{1,5},{5,9},{9,13},{2,6},{6,10},{10,14},{3,7},{... | collective-permute-start | bytes 294920 | tf_op jit(solution)/shard_map/ppermute | solution.py:20
  13.3 11.9 %collective-permute-start.1 = (bf16[1,32,1536]{2,1,0:T(8,128)(2,1)S(1)}, bf16[1,32,1536]{2,1,0:T(8,128)(2,1)S(1)}, u32[]{:S(2)}, u32[]{:S(2)}) collective-permute-start(bf16[1,32,1536]{2,1,0:T(8,128)(2,1)S(1)} %get-tuple-element.18), channel_id=1, source_target_pairs={{4,0},{8,4},{12,8},{5,1},{9,5},{13,9},{6,2},{10,6},{14,10},{7,3},{... | collective-permute-start | bytes 294920 | tf_op jit(solution)/shard_map/ppermute | solution.py:22
  16.3 0.7 copy-start.23
  16.3 0.8 copy-start.26
  16.3 1.2 copy-start.7
  17.4 108.2 %copy-start.24 = (pred[2,6]{0,1:T(8,128)(4,1)}, pred[2,6]{0,1:T(8,128)(4,1)S(1)}, u32[]{:S(2)}) copy-start(pred[2,6]{0,1:T(8,128)(4,1)S(1)} %copy.31) | copy-start | bytes 40
  21.8 2.6 %copy-start.9 = (f32[3,3,1536]{2,1,0:T(4,128)S(1)}, f32[3,3,1536]{2,1,0:T(4,128)}, u32[]{:S(2)}) copy-start(f32[3,3,1536]{2,1,0:T(4,128)} %param.18) | copy-start | bytes 165892
  22.8 113.2 %copy-start.22 = (pred[2,8]{0,1:T(8,128)(4,1)}, pred[2,8]{0,1:T(8,128)(4,1)S(1)}, u32[]{:S(2)}) copy-start(pred[2,8]{0,1:T(8,128)(4,1)S(1)} %copy.40) | copy-start | bytes 52
  25.2 1.0 copy-start.5
  26.3 145.3 %collective-permute-start.2 = (bf16[10,1,1536]{2,1,0:T(2,128)(2,1)S(1)}, bf16[10,1,1536]{2,1,0:T(2,128)(2,1)S(1)}, u32[]{:S(2)}, u32[]{:S(2)}) collective-permute-start(bf16[10,1,1536]{2,1,0:T(2,128)(2,1)S(1)} %get-tuple-element.16), channel_id=1, source_target_pairs={{0,1},{1,2},{2,3},{4,5},{5,6},{6,7},{8,9},{9,10},{10,11},{12,13},{... | collective-permute-start | bytes 92168 | tf_op jit(solution)/shard_map/ppermute | solution.py:20
  30.6 140.9 %collective-permute-start.3 = (bf16[10,1,1536]{2,1,0:T(2,128)(2,1)S(1)}, bf16[10,1,1536]{2,1,0:T(2,128)(2,1)}, u32[]{:S(2)}, u32[]{:S(2)}) collective-permute-start(bf16[10,1,1536]{2,1,0:T(2,128)(2,1)S(1)} %get-tuple-element.17), channel_id=1, source_target_pairs={{1,0},{2,1},{3,2},{5,4},{6,5},{7,6},{9,8},{10,9},{11,10},{13,12},{... | collective-permute-start | bytes 92168 | tf_op jit(solution)/shard_map/ppermute | solution.py:22
  98.6 23.4 %copy-start.3 = (bf16[2,128,12,128]{3,2,1,0:T(8,128)(2,1)S(1)}, bf16[2,128,12,128]{3,2,1,0:T(8,128)(2,1)}, u32[]{:S(2)}) copy-start(bf16[2,128,12,128]{3,2,1,0:T(8,128)(2,1)} %reshape_reshape.23) | copy-start | bytes 2359300
  125.6 10.4 %copy-start.1 = (f32[12,8,128,2,128]{4,2,3,1,0:T(8,128)}, f32[12,8,128,2,128]{4,2,3,1,0:T(8,128)S(1)}, u32[]{:S(2)}) copy-start(f32[12,8,128,2,128]{4,2,3,1,0:T(8,128)S(1)} %get-tuple-element.26) | copy-start | bytes 37748740
  139.3 21.2 %copy-start.4 = (bf16[4,128,12,128]{1,3,0,2:T(8,128)(2,1)S(1)}, bf16[4,128,12,128]{1,3,0,2:T(8,128)(2,1)}, u32[]{:S(2)}) copy-start(bf16[4,128,12,128]{1,3,0,2:T(8,128)(2,1)} %copy.38) | copy-start | bytes 4718596
  139.3 21.2 %copy-start.8 = (bf16[2,128,12,128]{1,3,0,2:T(8,128)(2,1)S(1)}, bf16[2,128,12,128]{1,3,0,2:T(8,128)(2,1)}, u32[]{:S(2)}) copy-start(bf16[2,128,12,128]{1,3,0,2:T(8,128)(2,1)} %copy.37) | copy-start | bytes 2359300
  152.0 8.5 %copy-start.19 = (f32[2,128,12]{1,0,2:T(2,128)S(1)}, f32[2,128,12]{1,0,2:T(2,128)}, u32[]{:S(2)}) copy-start(f32[2,128,12]{1,0,2:T(2,128)} %get-tuple-element.14) | copy-start | bytes 36868
  152.0 8.5 %copy-start.20 = (f32[2,128,12]{1,0,2:T(2,128)S(1)}, f32[2,128,12]{1,0,2:T(2,128)}, u32[]{:S(2)}) copy-start(f32[2,128,12]{1,0,2:T(2,128)} %get-tuple-element.15) | copy-start | bytes 36868
  152.0 8.5 %copy-start.21 = (f32[2,128,12]{1,0,2:T(2,128)S(1)}, f32[2,128,12]{1,0,2:T(2,128)}, u32[]{:S(2)}) copy-start(f32[2,128,12]{1,0,2:T(2,128)} %get-tuple-element.20) | copy-start | bytes 36868
  152.0 8.5 %copy-start.25 = (pred[2,6]{0,1:T(8,128)(4,1)S(1)}, pred[2,6]{0,1:T(8,128)(4,1)}, u32[]{:S(2)}) copy-start(pred[2,6]{0,1:T(8,128)(4,1)} %copy-done.24) | copy-start | bytes 40
  170.1 1.5 copy-start.10
  170.1 1.5 copy-start.11
  170.1 1.5 copy-start.12
  170.1 1.5 copy-start.13
  170.1 1.5 copy-start.14
  170.1 1.5 copy-start.15
  170.1 1.5 copy-start.16
  170.1 1.5 copy-start.17
  170.1 1.5 copy-start.18
Sparse Core Ops, SparseCore 0:
  9.7 42.3 all-gather.4
  54.4 38.5 all-gather.6
  94.5 27.4 all-gather.8
  123.4 28.5 all-gather.10
where the time goes:
time: 185 us; the launch traced here: 184 us
  waiting for transfers between devices  86.7 us (47%)
  local copies, waits for them, and re-layouts  27.6 us (15%)
  matrix products  26.7 us (14%)
  other arithmetic  20 us (11%)
  between operations  13.6 us (7%)
  starting transfers between devices  9.56 us (5%)
    all_gather x1, waiting for transfers between devices, body(): lax.all_gather(text_v, ('rows', 'cols'), axis=0, tiled=True)  36.5 us
    another operation x13, local copies, waits for them, and re-layouts, split_heads(): flat_rows.reshape(flat_rows.shape[:-1] + (flat_rows.shape[-1] // HEAD_DIM...  20.9 us
    all_gather x1, waiting for transfers between devices, body(): lax.all_gather(text_k, ('rows', 'cols'), axis=0, tiled=True)  20 us
    all_gather x1, waiting for transfers between devices, body(): piece_keys = lax.all_gather(as_blocks(k_stale), 'rows', axis=0, tiled=True)  16.1 us
    dot_general x2, matrix products, attend(): jnp.einsum('bhqnk,nkhd->bqhd', weights, value_blocks, preferred_element_t...  15.8 us
    reduce_sum x2, other arithmetic, attend(): jnp.sum(weights.astype(jnp.float32), axis=(3, 4))  13 us
    all_gather x1, waiting for transfers between devices, body(): lax.all_gather(as_blocks(v_stale), 'rows', axis=0, tiled=True)  12.7 us
    dot_general x2, matrix products, attend(): jnp.einsum('bqhd,nkhd->bhqnk', queries, key_blocks, preferred_element_typ...  10.9 us
  transfers between devices with their start and end apart: 8, of which 4 were waited for; matrix products, arithmetic and copies ran while one was open for 36% of the time, Pallas kernels for 0%

commit v1 on v0

--- a/solution.py
+++ b/solution.py
@@ -93,7 +93,17 @@
     chosen = jnp.where(
         wanted >= blocks_here, fetch_rows[jnp.clip(wanted - blocks_here, 0, fetch_count - 1)], -1
     )
-    piece_keys = lax.all_gather(as_blocks(k_stale), "rows", axis=0, tiled=True)
+    x = as_blocks(k_stale)
+    ways = lax.axis_size("rows")
+    up = [(d, (d + 1) % ways) for d in range(ways)]
+    down = [(d, (d - 1) % ways) for d in range(ways)]
+    earlier, later = ([x], [x])
+    for _ in range(ways // 2):
+        earlier.append(lax.ppermute(earlier[-1], "rows", up))
+    for _ in range((ways - 1) // 2):
+        later.append(lax.ppermute(later[-1], "rows", down))
+    line = jnp.concatenate([*earlier[::-1], *later[1:]], axis=0)
+    piece_keys = jnp.roll(line, (lax.axis_index("rows") - ways // 2) * x.shape[0], axis=0)
     piece_values = lax.all_gather(as_blocks(v_stale), "rows", axis=0, tiled=True)
     piece_count = piece_keys.shape[0]
     block_rows = jnp.arange(piece_count, dtype=jnp.int32)

time: 185 us -> 157 us (0.85)
  waiting for transfers between devices: 86.7 us -> 48.5 us
  local copies, waits for them, and re-layouts: 27.6 us -> 36.8 us
  other arithmetic: 20 us -> 14.8 us
  starting transfers between devices: 9.56 us -> 13.5 us
  matrix products: 26.7 us -> 28.9 us
    all_gather x1, waiting for transfers between devices: 20 us -> 0.01 us  [body(): lax.all_gather(text_k, ('rows', 'cols'), axis=0, tiled=True)]
    all_gather x1 -> x0, waiting for transfers between devices: 16.1 us -> none  [body(): piece_keys = lax.all_gather(as_blocks(k_stale), 'rows', axis=0, tiled=True)]
    ppermute x0 -> x3, waiting for transfers between devices: none -> 9.09 us  [the longest x2 9.08 us: body(): earlier.append(lax.ppermute(earlier[-1], 'rows', up))]
    all_gather x1, waiting for transfers between devices: 36.5 us -> 30.6 us  [body(): lax.all_gather(text_v, ('rows', 'cols'), axis=0, tiled=True)]
    all_gather x1, waiting for transfers between devices: 12.7 us -> 7.43 us  [body(): lax.all_gather(as_blocks(v_stale), 'rows', axis=0, tiled=True)]
    ppermute x0 -> x3, starting transfers between devices: none -> 4.81 us  [the longest x2 2.88 us: body(): earlier.append(lax.ppermute(earlier[-1], 'rows', up))]
    reduce_sum x2, other arithmetic: 13 us -> 8.42 us  [attend(): jnp.sum(weights.astype(jnp.float32), axis=(3, 4))]
    another operation x13, local copies, waits for them, and re-layouts: 20.9 us -> 24.9 us  [split_heads(): flat_rows.reshape(flat_rows.shape[:-1] + (flat_rows.shape[-1] // HEAD_DIM...]
  transfers between devices with their start and end apart: 8 -> 10, of which waited for: 4 -> 3; matrix products, arithmetic and copies ran while one was open for 36% -> 48% of each run, Pallas kernels for 0% -> 0%
where the time goes in v1:
time: 157 us; the launch traced here: 156 us
  waiting for transfers between devices  48.5 us (31%)
  local copies, waits for them, and re-layouts  36.8 us (23%)
  matrix products  28.9 us (18%)
  other arithmetic  14.8 us (9%)
  between operations  13.7 us (9%)
  starting transfers between devices  13.5 us (9%)
    all_gather x1, waiting for transfers between devices, body(): lax.all_gather(text_v, ('rows', 'cols'), axis=0, tiled=True)  30.6 us
    another operation x13, local copies, waits for them, and re-layouts, split_heads(): flat_rows.reshape(flat_rows.shape[:-1] + (flat_rows.shape[-1] // HEAD_DIM...  24.9 us
    dot_general x2, matrix products, attend(): jnp.einsum('bhqnk,nkhd->bqhd', weights, value_blocks, preferred_element_t...  15.8 us
    dot_general x2, matrix products, attend(): jnp.einsum('bqhd,nkhd->bhqnk', queries, key_blocks, preferred_element_typ...  13.2 us
    ppermute x2, waiting for transfers between devices, body(): earlier.append(lax.ppermute(earlier[-1], 'rows', up))  9.08 us
    reduce_sum x2, other arithmetic, attend(): jnp.sum(weights.astype(jnp.float32), axis=(3, 4))  8.42 us
    all_gather x1, waiting for transfers between devices, body(): lax.all_gather(as_blocks(v_stale), 'rows', axis=0, tiled=True)  7.43 us
    ppermute x2, starting transfers between devices, extended(): lax.ppermute(tail, axis, [(i, (i + 1) % count) for i in range(ends)])  6.07 us
  transfers between devices with their start and end apart: 10, of which 3 were waited for; matrix products, arithmetic and copies ran while one was open for 48% of the time, Pallas kernels for 0%

profile of v1, /device:TPU:0, one launch (start us, length us, event | category | flops | bytes accessed | tf_op | source)
XLA Modules:
  0.0 156.3 jit_solution(17430815000784801664)
XLA Ops:
  6.5 0.7 all-gather.4.cloned.1.call-update
  7.3 0.0 all-gather.6.cloned.1.call-start
  7.3 0.7 all-gather.6.cloned.1.call-update
  8.0 0.0 all-gather.8.cloned.1.call-start
  8.1 1.6 %reshape_reshape.26 = bf16[2,128,12,128]{3,2,1,0:T(8,128)(2,1)S(1)} reshape(bf16[8,32,1536]{2,1,0:T(8,128)(2,1)} %param.14) | data formatting | bytes 1572864 | tf_op jit(solution)/shard_map/reshape;reshape | solution.py:30
  9.7 1.1 copy.44
  10.8 0.5 collective-permute-start
  11.3 1.9 %collective-permute-start.2 = (bf16[2,128,12,128]{3,1,0,2:T(8,128)(2,1)}, bf16[2,128,12,128]{3,1,0,2:T(8,128)(2,1)}, u32[]{:S(2)}, u32[]{:S(2)}) collective-permute-start(bf16[2,128,12,128]{3,1,0,2:T(8,128)(2,1)} %copy.44), channel_id=1, source_target_pairs={{0,12},{4,0},{8,4},{12,8},{1,13},{5,1},{9,5},{13,9},{2,14},{6,2},{... | collective-permute-start | bytes 2359304 | tf_op jit(solution)/shard_map/ppermute | solution.py:104
  13.2 2.6 %collective-permute-start.3 = (bf16[1,32,1536]{2,1,0:T(8,128)(2,1)S(1)}, bf16[1,32,1536]{2,1,0:T(8,128)(2,1)S(1)}, u32[]{:S(2)}, u32[]{:S(2)}) collective-permute-start(bf16[1,32,1536]{2,1,0:T(8,128)(2,1)S(1)} %get-tuple-element.19), channel_id=1, source_target_pairs={{0,4},{4,8},{8,12},{1,5},{5,9},{9,13},{2,6},{6,10},{10,14},{3,7},{... | collective-permute-start | bytes 294920 | tf_op jit(solution)/shard_map/ppermute | solution.py:20
  15.8 1.3 collective-permute-start.4
  17.1 1.6 %reshape_reshape.27 = bf16[2,128,12,128]{3,2,1,0:T(8,128)(2,1)S(1)} reshape(bf16[8,32,1536]{2,1,0:T(8,128)(2,1)} %param.15) | data formatting | bytes 1572864 | tf_op jit(solution)/shard_map/reshape;reshape | solution.py:30
  18.8 0.0 copy-start.18
  18.8 1.1 copy.49
  19.9 0.0 all-gather.8.cloned.1.call-update
  19.9 0.0 copy-start.20
  19.9 0.5 reshape_reshape.24
  20.5 0.1 reshape.56
  20.6 0.6 gather_fusion
  21.3 0.1 reshape.55
  21.4 0.1 compare_reduce_fusion
  21.5 0.1 copy.43
  21.6 2.4 %reshape_reshape.23 = bf16[2,128,12,128]{3,2,1,0:T(8,128)(2,1)} reshape(bf16[8,32,1536]{2,1,0:T(8,128)(2,1)} %param.11) | data formatting | bytes 1572864 | tf_op jit(solution)/shard_map/reshape;reshape | solution.py:30
  24.0 0.1 compare_reduce_fusion.2
  24.1 0.1 compare_reduce_fusion.1
  24.1 0.1 pad_add_fusion
  24.2 0.7 copy.34
  24.9 2.4 %reshape_reshape.21 = bf16[2,128,12,128]{3,2,1,0:T(8,128)(2,1)} reshape(bf16[8,32,1536]{2,1,0:T(8,128)(2,1)} %param.12) | data formatting | bytes 1572864 | tf_op jit(solution)/shard_map/reshape;reshape | solution.py:30
  27.3 2.4 %copy.36 = bf16[2,128,12,128]{3,1,0,2:T(8,128)(2,1)} copy(bf16[2,128,12,128]{3,2,1,0:T(8,128)(2,1)} %reshape_reshape.21) | data formatting | bytes 1572864 | tf_op jit(solution)/shard_map/reshape;reshape | solution.py:30
  29.7 1.5 copy.40
  31.2 0.7 slice_reduce_fusion.8
  31.9 0.0 collective-permute-done.3
  32.0 0.0 collective-permute-done
  32.0 2.4 %collective-permute-start.1 = (bf16[2,128,12,128]{3,1,0,2:T(8,128)(2,1)}, bf16[2,128,12,128]{3,1,0,2:T(8,128)(2,1)S(1)}, u32[]{:S(2)}, u32[]{:S(2)}) collective-permute-start(bf16[2,128,12,128]{3,1,0,2:T(8,128)(2,1)} %collective-permute-done), channel_id=1, source_target_pairs={{0,4},{4,8},{8,12},{12,0},{1,5},{5,9},{9,13},{13,1},{2,6},{6,10},{... | collective-permute-start | bytes 2359304 | tf_op jit(solution)/shard_map/ppermute | solution.py:102
  34.4 0.1 constant_dynamic-update-slice_fusion.9
  34.5 0.0 collective-permute-done.4
  34.5 0.1 fusion.38
  34.6 3.5 %collective-permute-start.5 = (bf16[10,1,1536]{2,1,0:T(2,128)(2,1)S(1)}, bf16[10,1,1536]{2,1,0:T(2,128)(2,1)S(1)}, u32[]{:S(2)}, u32[]{:S(2)}) collective-permute-start(bf16[10,1,1536]{2,1,0:T(2,128)(2,1)S(1)} %get-tuple-element.16), channel_id=1, source_target_pairs={{0,1},{1,2},{2,3},{4,5},{5,6},{6,7},{8,9},{9,10},{10,11},{12,13},{... | collective-permute-start | bytes 92168 | tf_op jit(solution)/shard_map/ppermute | solution.py:20
  38.1 1.3 collective-permute-start.6
  39.4 9.1 %collective-permute-done.1 = bf16[2,128,12,128]{3,1,0,2:T(8,128)(2,1)S(1)} collective-permute-done((bf16[2,128,12,128]{3,1,0,2:T(8,128)(2,1)}, bf16[2,128,12,128]{3,1,0,2:T(8,128)(2,1)S(1)}, u32[]{:S(2)}, u32[]{:S(2)}) %collective-permute-start.1) | collective-permute-done | bytes 786464 | tf_op jit(solution)/shard_map/ppermute | solution.py:102
  48.5 0.1 constant_dynamic-update-slice_fusion.7
  48.5 1.3 constant_dynamic-update-slice_fusion.6
  49.8 0.3 constant_dynamic-update-slice_fusion.5
  50.1 1.3 constant_dynamic-update-slice_fusion.4
  51.4 0.1 constant_dynamic-update-slice_fusion.3
  51.5 1.4 constant_dynamic-update-slice_fusion.2
  52.9 0.3 constant_dynamic-update-slice_fusion.1
  53.1 1.3 constant_dynamic-update-slice_fusion
  54.4 5.8 %fusion = (f32[2,12,128]{2,0,1:T(2,128)S(1)}, f32[12,8,128,2,128]{4,2,3,1,0:T(8,128)}) fusion(pred[2,8]{0,1:T(8,128)(4,1)S(1)} %copy.43, bf16[2,128,12,128,1]{3,2,1,0,4:T(8,128)(2,1)S(1)} %bitcast.100, bf16[16,128,12,128]{3,1,0,2:T(8,128)(2,1)S(1)} %constant_dynamic-update-slice_fusion, s32[]{:T(128)S(6)} %select_n.43), kind=kOutput, calls=%fused_computation.4 | convolution fusion | flops 814740480 | bytes 16790532 | tf_op jit(solution)/shard_map/bqhd,nkhd->bhqnk/dot_general | solution.py:35
  60.2 2.9 %reshape.71 = bf16[4,128,12,128]{3,2,1,0:T(8,128)(2,1)S(1)} reshape(bf16[512,1536]{1,0:T(8,128)(2,1)} %all-gather.4.cloned.1.call-done) | data formatting | bytes 3145728 | tf_op jit(solution)/shard_map/reshape;reshape | solution.py:30
  63.1 1.6 copy.37
  64.7 30.6 %all-gather.6.cloned.1.call-done = bf16[512,1536]{1,0:T(8,128)(2,1)} async-done(((bf16[32,1536]{1,0:T(8,128)(2,1)}), bf16[512,1536]{1,0:T(8,128)(2,1)}) %all-gather.6.cloned.1.call-update) | async-done | bytes 1572880 | tf_op jit(solution)/shard_map/all_gather | solution.py:66
  95.2 2.9 %reshape.72 = bf16[4,128,12,128]{3,2,1,0:T(8,128)(2,1)S(1)} reshape(bf16[512,1536]{1,0:T(8,128)(2,1)} %all-gather.6.cloned.1.call-done) | data formatting | bytes 3145728 | tf_op jit(solution)/shard_map/reshape;reshape | solution.py:30
  98.2 2.8 %copy.41 = bf16[4,128,12,128]{1,3,0,2:T(8,128)(2,1)} copy(bf16[4,128,12,128]{3,2,1,0:T(8,128)(2,1)S(1)} %reshape.72) | data formatting | bytes 3145728 | tf_op jit(solution)/shard_map/reshape;reshape | solution.py:30
  100.9 7.4 %fusion.1 = (f32[2,12,128]{2,0,1:T(2,128)S(1)}, f32[12,6,128,2,128]{4,2,3,1,0:T(8,128)}) fusion(pred[2,6]{0,1:T(8,128)(4,1)S(1)} %copy-done.19, bf16[2,128,12,128,1]{3,2,1,0,4:T(8,128)(2,1)S(1)} %bitcast.101, bf16[4,128,12,128]{3,1,0,2:T(8,128)(2,1)} %copy.37, bf16[2,128,12,128]{3,1,0,2:T(8,128)(2,1)} %copy.36), kind=kOutput, calls=%fused_computation.8 | convolution fusion | flops 615773184 | bytes 12595212 | tf_op jit(solution)/shard_map/bqhd,nkhd->bhqnk/dot_general | solution.py:35
  108.3 0.0 slice-start.2
  108.3 5.8 %convert_reduce_fusion.1 = f32[2,12,128]{2,0,1:T(2,128)S(1)} fusion(f32[2,12,128]{2,0,1:T(2,128)S(1)} %get-tuple-element.21, f32[12,6,128,2,128]{4,2,3,1,0:T(8,128)} %get-tuple-element.24, pred[2,6]{0,1:T(8,128)(4,1)S(1)} %copy-done.19), kind=kLoop, calls=%fused_computation.6 | loop fusion | flops 14152704 | bytes 9461772 | tf_op jit(solution)/shard_map/reduce_sum | solution.py:42
  114.2 2.6 %convert_reduce_fusion = f32[2,12,128]{2,0,1:T(2,128)S(1)} fusion(f32[2,12,128]{2,0,1:T(2,128)S(1)} %get-tuple-element.22, f32[12,8,128,2,128]{4,2,3,1,0:T(8,128)S(1)} %bitcast.99, pred[2,8]{0,1:T(8,128)(4,1)S(1)} %copy.43), kind=kLoop, calls=%fused_computation.2 | loop fusion | flops 18871296 | bytes 12607504 | tf_op jit(solution)/shard_map/reduce_sum | solution.py:42
  116.8 7.4 %all-gather.8.cloned.1.call-done = bf16[8,128,12,128]{3,1,0,2:T(8,128)(2,1)} async-done(((bf16[2,128,12,128]{3,1,0,2:T(8,128)(2,1)}), bf16[8,128,12,128]{3,1,0,2:T(8,128)(2,1)}) %all-gather.8.cloned.1.call-update) | async-done | bytes 3145744 | tf_op jit(solution)/shard_map/all_gather | solution.py:107
  124.3 8.4 %fusion.2 = f32[12,2,128,128,1]{2,3,1,4,0:T(8,128)S(1)} fusion(bf16[8,128,12,128]{3,1,0,2:T(8,128)(2,1)} %all-gather.8.cloned.1.call-done, f32[12,8,128,2,128]{4,2,3,1,0:T(8,128)} %get-tuple-element.26, f32[2,12,128]{2,0,1:T(2,128)S(1)} %get-tuple-element.22, pred[2,8]{0,1:T(8,128)(4,1)S(1)} %copy.43), kind=kOutput, calls=%fused_computation.9 | convolution fusion | flops 817889280 | bytes 17313808 | tf_op jit(solution)/shard_map/bhqnk,nkhd->bqhd/dot_general | solution.py:43
  132.7 7.3 %fusion.15 = f32[2,128,12,128]{1,3,0,2:T(8,128)} fusion(f32[12,2,128,128,1]{2,3,1,4,0:T(8,128)S(1)} %fusion.2, bf16[4,128,12,128]{1,3,0,2:T(8,128)(2,1)S(1)} %copy-done.4, bf16[2,128,12,128]{1,3,0,2:T(8,128)(2,1)S(1)} %copy-done.8, f32[2,128,12]{1,0,2:T(2,128)S(1)} %get-tuple-element.14, f32[2,128,12]{1,0,2:T(2,128)S(1)} %get-tuple-element.15, ...), kind=kOutput, calls=%fused_computation.28 | convolution fusion | flops 619708416 | bytes 14991372 | tf_op jit(solution)/shard_map/bhqnk,nkhd->bqhd/dot_general | solution.py:43
  140.1 2.2 %copy.52 = f32[2,128,12,128]{3,2,1,0:T(8,128)S(1)} copy(f32[2,128,12,128]{1,3,0,2:T(8,128)} %fusion.15) | data formatting | bytes 3145728 | tf_op jit(solution)/shard_map/div | solution.py:113
  142.2 0.0 copy-start.3
  142.3 1.4 reshape.53
  143.8 6.0 %add_add_fusion = f32[8,32,1536]{2,1,0:T(8,128)} fusion(f32[8,32,1536]{2,1,0:T(8,128)} %reshape.53, bf16[8,32,1536]{2,1,0:T(8,128)(2,1)S(1)} %copy-done.3, bf16[10,32,1536]{2,1,0:T(8,128)(2,1)} %copy-done.5, bf16[10,1,1536]{2,1,0:T(2,128)(2,1)} %collective-permute-done.6, bf16[10,1,1536]{2,1,0:T(2,128)(2,1)S(1)} %collective-permute-done.5, ...), kind=kLoop, calls=%fused_computation.31 | loop fusion | flops 20054016 | bytes 5228544 | tf_op jit(solution)/shard_map/add | solution.py:122
  (59 shorter events, 0.2 us)
Async XLA Ops:
  6.5 14.1 %copy-start = (s32[1,1,2]{2,1,0:T(1,128)S(1)}, s32[1,1,2]{2,1,0:T(1,128)}, u32[]{:S(2)}) copy-start(s32[1,1,2]{2,1,0:T(1,128)} %param.19) | copy-start | bytes 28
  6.5 6.7 %copy-start.2 = (bf16[8,32,1536]{2,1,0:T(8,128)(2,1)S(1)}, bf16[8,32,1536]{2,1,0:T(8,128)(2,1)}, u32[]{:S(2)}) copy-start(bf16[8,32,1536]{2,1,0:T(8,128)(2,1)} %param.13) | copy-start | bytes 2359300
  6.5 53.7 %all-gather.4.cloned.1.call-start = ((), (), s32[]{:S(2)}) async-start(), calls=%async_computation | async-start | bytes 1671168 | tf_op jit(solution)/shard_map/all_gather | solution.py:65
  7.3 88.0 %all-gather.6.cloned.1.call-start = ((), (), s32[]{:S(2)}) async-start(), calls=%async_computation.1 | async-start | bytes 1671168 | tf_op jit(solution)/shard_map/all_gather | solution.py:66
  8.0 116.3 %all-gather.8.cloned.1.call-start = ((), (), s32[]{:S(2)}) async-start(), calls=%async_computation.2 | async-start | bytes 3932160 | tf_op jit(solution)/shard_map/all_gather | solution.py:107
  10.8 21.1 %collective-permute-start = (bf16[2,128,12,128]{3,1,0,2:T(8,128)(2,1)}, bf16[2,128,12,128]{3,1,0,2:T(8,128)(2,1)}, u32[]{:S(2)}, u32[]{:S(2)}) collective-permute-start(bf16[2,128,12,128]{3,1,0,2:T(8,128)(2,1)} %copy.44), channel_id=1, source_target_pairs={{0,4},{4,8},{8,12},{12,0},{1,5},{5,9},{9,13},{13,1},{2,6},{6,10},{... | collective-permute-start | bytes 2359304 | tf_op jit(solution)/shard_map/ppermute | solution.py:102
  11.3 38.8 %collective-permute-start.2 = (bf16[2,128,12,128]{3,1,0,2:T(8,128)(2,1)}, bf16[2,128,12,128]{3,1,0,2:T(8,128)(2,1)}, u32[]{:S(2)}, u32[]{:S(2)}) collective-permute-start(bf16[2,128,12,128]{3,1,0,2:T(8,128)(2,1)} %copy.44), channel_id=1, source_target_pairs={{0,12},{4,0},{8,4},{12,8},{1,13},{5,1},{9,5},{13,9},{2,14},{6,2},{... | collective-permute-start | bytes 2359304 | tf_op jit(solution)/shard_map/ppermute | solution.py:104
  13.2 18.7 %collective-permute-start.3 = (bf16[1,32,1536]{2,1,0:T(8,128)(2,1)S(1)}, bf16[1,32,1536]{2,1,0:T(8,128)(2,1)S(1)}, u32[]{:S(2)}, u32[]{:S(2)}) collective-permute-start(bf16[1,32,1536]{2,1,0:T(8,128)(2,1)S(1)} %get-tuple-element.19), channel_id=1, source_target_pairs={{0,4},{4,8},{8,12},{1,5},{5,9},{9,13},{2,6},{6,10},{10,14},{3,7},{... | collective-permute-start | bytes 294920 | tf_op jit(solution)/shard_map/ppermute | solution.py:20
  15.8 18.6 %collective-permute-start.4 = (bf16[1,32,1536]{2,1,0:T(8,128)(2,1)S(1)}, bf16[1,32,1536]{2,1,0:T(8,128)(2,1)S(1)}, u32[]{:S(2)}, u32[]{:S(2)}) collective-permute-start(bf16[1,32,1536]{2,1,0:T(8,128)(2,1)S(1)} %get-tuple-element.18), channel_id=1, source_target_pairs={{4,0},{8,4},{12,8},{5,1},{9,5},{13,9},{6,2},{10,6},{14,10},{7,3},{... | collective-permute-start | bytes 294920 | tf_op jit(solution)/shard_map/ppermute | solution.py:22
  18.8 1.7 %copy-start.18 = (s32[2,1,2]{2,1,0:T(1,128)S(1)}, s32[2,1,2]{2,1,0:T(1,128)}, u32[]{:S(2)}) copy-start(s32[2,1,2]{2,1,0:T(1,128)} %param.20) | copy-start | bytes 52
  19.9 4.1 %copy-start.20 = (s32[2,1,2]{2,1,0:T(1,128)S(1)}, s32[2,1,2]{2,1,0:T(1,128)}, u32[]{:S(2)}) copy-start(s32[2,1,2]{2,1,0:T(1,128)} %param.21) | copy-start | bytes 52
  24.9 6.3 %copy-start.9 = (f32[3,3,1536]{2,1,0:T(4,128)S(1)}, f32[3,3,1536]{2,1,0:T(4,128)}, u32[]{:S(2)}) copy-start(f32[3,3,1536]{2,1,0:T(4,128)} %param.18) | copy-start | bytes 165892
  32.0 16.5 %collective-permute-start.1 = (bf16[2,128,12,128]{3,1,0,2:T(8,128)(2,1)}, bf16[2,128,12,128]{3,1,0,2:T(8,128)(2,1)S(1)}, u32[]{:S(2)}, u32[]{:S(2)}) collective-permute-start(bf16[2,128,12,128]{3,1,0,2:T(8,128)(2,1)} %collective-permute-done), channel_id=1, source_target_pairs={{0,4},{4,8},{8,12},{12,0},{1,5},{5,9},{9,13},{13,1},{2,6},{6,10},{... | collective-permute-start | bytes 2359304 | tf_op jit(solution)/shard_map/ppermute | solution.py:102
  34.5 14.0 %copy-start.5 = (bf16[10,32,1536]{2,1,0:T(8,128)(2,1)}, bf16[10,32,1536]{2,1,0:T(8,128)(2,1)S(1)}, u32[]{:S(2)}) copy-start(bf16[10,32,1536]{2,1,0:T(8,128)(2,1)S(1)} %constant_dynamic-update-slice_fusion.8) | copy-start | bytes 2949124
  34.6 109.1 %collective-permute-start.5 = (bf16[10,1,1536]{2,1,0:T(2,128)(2,1)S(1)}, bf16[10,1,1536]{2,1,0:T(2,128)(2,1)S(1)}, u32[]{:S(2)}, u32[]{:S(2)}) collective-permute-start(bf16[10,1,1536]{2,1,0:T(2,128)(2,1)S(1)} %get-tuple-element.16), channel_id=1, source_target_pairs={{0,1},{1,2},{2,3},{4,5},{5,6},{6,7},{8,9},{9,10},{10,11},{12,13},{... | collective-permute-start | bytes 92168 | tf_op jit(solution)/shard_map/ppermute | solution.py:20
  38.1 105.6 %collective-permute-start.6 = (bf16[10,1,1536]{2,1,0:T(2,128)(2,1)S(1)}, bf16[10,1,1536]{2,1,0:T(2,128)(2,1)}, u32[]{:S(2)}, u32[]{:S(2)}) collective-permute-start(bf16[10,1,1536]{2,1,0:T(2,128)(2,1)S(1)} %get-tuple-element.17), channel_id=1, source_target_pairs={{1,0},{2,1},{3,2},{5,4},{6,5},{7,6},{9,8},{10,9},{11,10},{13,12},{... | collective-permute-start | bytes 92168 | tf_op jit(solution)/shard_map/ppermute | solution.py:22
  51.5 2.9 %copy-start.6 = (bf16[2,128,12,128]{3,2,1,0:T(8,128)(2,1)S(1)}, bf16[2,128,12,128]{3,2,1,0:T(8,128)(2,1)}, u32[]{:S(2)}) copy-start(bf16[2,128,12,128]{3,2,1,0:T(8,128)(2,1)} %reshape_reshape.23) | copy-start | bytes 2359300
  98.1 2.8 %copy-start.7 = (bf16[2,128,12,128]{3,2,1,0:T(8,128)(2,1)S(1)}, bf16[2,128,12,128]{3,2,1,0:T(8,128)(2,1)}, u32[]{:S(2)}) copy-start(bf16[2,128,12,128]{3,2,1,0:T(8,128)(2,1)} %reshape_reshape.23) | copy-start | bytes 2359300
  98.1 2.8 %copy-start.19 = (pred[2,6]{0,1:T(8,128)(4,1)S(1)}, pred[2,6]{0,1:T(8,128)(4,1)}, u32[]{:S(2)}) copy-start(pred[2,6]{0,1:T(8,128)(4,1)} %copy.34) | copy-start | bytes 40
  100.9 13.2 %slice-start = ((s8[12582912]{0:T(1024)(128)(4,1)}), s8[4194304]{0:T(1024)(128)(4,1)S(1)}, s32[]{:S(2)}) async-start(s8[12582912]{0:T(1024)(128)(4,1)} %bitcast.98), calls=%async_computation.3 | async-start | bytes 8388608
  100.9 13.3 %slice-start.1 = ((s8[12582912]{0:T(1024)(128)(4,1)}), s8[4194304]{0:T(1024)(128)(4,1)S(1)}, s32[]{:S(2)}) async-start(s8[12582912]{0:T(1024)(128)(4,1)} %bitcast.98), calls=%async_computation.4 | async-start | bytes 8388608
  108.3 5.9 %slice-start.2 = ((s8[12582912]{0:T(1024)(128)(4,1)}), s8[4194304]{0:T(1024)(128)(4,1)S(1)}, s32[]{:S(2)}) async-start(s8[12582912]{0:T(1024)(128)(4,1)} %bitcast.98), calls=%async_computation.5 | async-start | bytes 8388608
  116.8 15.9 %copy-start.4 = (bf16[4,128,12,128]{1,3,0,2:T(8,128)(2,1)S(1)}, bf16[4,128,12,128]{1,3,0,2:T(8,128)(2,1)}, u32[]{:S(2)}) copy-start(bf16[4,128,12,128]{1,3,0,2:T(8,128)(2,1)} %copy.41) | copy-start | bytes 4718596
  116.8 15.9 %copy-start.8 = (bf16[2,128,12,128]{1,3,0,2:T(8,128)(2,1)S(1)}, bf16[2,128,12,128]{1,3,0,2:T(8,128)(2,1)}, u32[]{:S(2)}) copy-start(bf16[2,128,12,128]{1,3,0,2:T(8,128)(2,1)} %copy.40) | copy-start | bytes 2359300
  142.2 1.5 copy-start.3
  142.2 1.5 copy-start.10
  142.2 1.5 copy-start.11
  142.3 1.5 copy-start.12
  142.3 1.5 copy-start.13
  142.3 1.5 copy-start.14
  142.3 1.5 copy-start.15
  142.3 1.5 copy-start.16
  142.3 1.5 copy-start.17
  143.7 6.1 %copy-start.1 = (s32[1,1,2]{2,1,0:T(1,128)S(1)}, s32[1,1,2]{2,1,0:T(1,128)}, u32[]{:S(2)}) copy-start(s32[1,1,2]{2,1,0:T(1,128)} %param.19) | copy-start | bytes 28
Sparse Core Ops, SparseCore 0:
  9.7 44.5 all-gather.3
  56.6 38.5 all-gather.5
  96.8 27.4 all-gather.7
